TPU v7x, 32 devices: a whole 2x2x4 slice. The times are simulated.
32 devices in a mesh: dp: 8 (over y, x, core), mp: 4 (over z).
Axes of the slice: x: 2, y: 2, z: 4, core: 2. Of those that a mesh axis runs over, the one named last changes fastest.
Arguments:
- pre: bfloat16 [1024, 12288], P('dp', 'mp'), may hold values from -32 to 32
- weight: float32 [6144, 12288], P('dp', 'mp'), may hold values from -0.0546875 to 0.0546875
- target: bfloat16 [6144, 1024], P('dp'), may hold values from -100 to 100
Outputs:
- update: float32 [6144, 12288], P('dp', 'mp')
All inputs are finite; a program needn't handle non-finite values.
Results may differ from a plain program's by a relative error of at most 0.0003.
The roundings to bfloat16 on the way count: a program that leaves them out, or rounds other values in their place, can miss the bound.
Values may be sent and summed in bfloat16 or wider, within the bound.
A program may use at most 64 MiB of HBM per device.

v0:
```python
import jax
import jax.numpy as jnp
from jax import lax
from jax.sharding import PartitionSpec as P

radius = 0.005
epsilon = 1e-06


def on_device(pre, weight, target):
    hidden = jax.nn.gelu(pre.astype(jnp.float32), approximate=False).astype(jnp.bfloat16)
    everyone = lax.all_gather(hidden, "dp", axis=0, tiled=True)
    entries = weight.shape[0] * weight.shape[1] * lax.axis_size("dp") * lax.axis_size("mp")

    def residual_of(matrix):
        partial_out = lax.dot_general(
            matrix, everyone, (((1,), (1,)), ((), ())), preferred_element_type=jnp.float32
        )
        summed = lax.psum(partial_out, "mp")
        result = (summed - target.astype(jnp.float32)).astype(jnp.bfloat16)
        return result

    resid = residual_of(weight.astype(jnp.bfloat16))
    ascent = jnp.dot(resid, everyone, preferred_element_type=jnp.float32)
    ascent_ms = lax.psum(jnp.sum(ascent * ascent), ("dp", "mp")) / entries
    perturbed = (weight + radius * jnp.tanh(ascent / jnp.sqrt(ascent_ms + epsilon))).astype(
        jnp.bfloat16
    )
    resid_two = residual_of(perturbed)
    descent = jnp.dot(resid_two, everyone, preferred_element_type=jnp.float32)
    descent_ms = lax.psum(jnp.sum(descent * descent), ("dp", "mp")) / entries
    return descent / jnp.sqrt(descent_ms + epsilon)


def solution(mesh):
    return jax.shard_map(
        on_device,
        mesh=mesh,
        in_specs=(P("dp", "mp"), P("dp", "mp"), P("dp", None)),
        out_specs=P("dp", "mp"),
        check_vma=False,
    )
```

profile of v0, /device:TPU:0, one launch (start us, length us, event | category | flops | bytes accessed | tf_op | source)
XLA Modules:
  0.0 443.9 jit_solution(3158897468256516652)
XLA Ops:
  6.5 0.0 all-gather.2.cloned.1.call-start
  6.5 5.1 %fusion.9 = bf16[128,3072]{1,0:T(8,128)(2,1)} fusion(bf16[128,3072]{1,0:T(8,128)(2,1)} %param.3), kind=kLoop, calls=%fused_computation.16 | loop fusion | flops 25952256 | bytes 1572864 | tf_op jit(solution)/shard_map/convert_element_type | solution.py:11
  11.7 0.0 all-gather.2.cloned.1.call-update
  11.7 0.0 all-reduce.3.cloned.1.call-start
  11.8 48.3 %all-gather.2.cloned.1.call-done = bf16[1024,3072]{1,0:T(8,128)(2,1)} async-done(((bf16[128,3072]{1,0:T(8,128)(2,1)}), bf16[1024,3072]{1,0:T(8,128)(2,1)}) %all-gather.2.cloned.1.call-update) | async-done | bytes 6291472 | tf_op jit(solution)/shard_map/all_gather | solution.py:12
  60.1 11.1 %fusion.5 = f32[768,1024]{1,0:T(8,128)} fusion(bf16[1024,3072]{1,0:T(8,128)(2,1)} %all-gather.2.cloned.1.call-done, f32[768,3072]{1,0:T(8,128)} %param.4), kind=kOutput, calls=%fused_computation.14 | convolution fusion | flops 4834197504 | bytes 18874368 | tf_op jit(solution)/shard_map/dot_general | solution.py:16
  71.2 0.0 copy-start
  71.2 0.0 all-reduce.3.cloned.1.call-update
  71.2 0.0 all-reduce.5.cloned.1.call-start
  71.2 121.2 %all-reduce.3.cloned.1.call-done = f32[768,1024]{1,0:T(8,128)} async-done(((f32[768,1024]{1,0:T(8,128)}), f32[768,1024]{1,0:T(8,128)}) %all-reduce.3.cloned.1.call-update) | async-done | bytes 3145744 | tf_op jit(solution)/shard_map/psum | solution.py:19
  192.4 0.0 copy-done
  192.4 11.1 %multiply_reduce_fusion.1 = (f32[]{:T(128)}, f32[768,3072]{1,0:T(8,128)}) fusion(bf16[1024,3072]{1,0:T(8,128)(2,1)} %all-gather.2.cloned.1.call-done, f32[768,1024]{1,0:T(8,128)} %all-reduce.3.cloned.1.call-done, bf16[768,1024]{1,0:T(8,128)(2,1)S(1)} %copy-done), kind=kOutput, calls=%fused_computation.2 | convolution fusion | flops 4838916096 | bytes 20447236 | tf_op jit(solution)/shard_map/dot_general | solution.py:24
  203.5 39.6 %psum.29 = f32[]{:T(128)} all-reduce(f32[]{:T(128)} %get-tuple-element.5), channel_id=1, replica_groups=mesh['dp'=8,'mp'=4] {'dp','mp'}, use_global_device_ids=true, to_apply=%region_2.0 | all-reduce | flops 1 | bytes 8 | tf_op jit(solution)/shard_map/psum | solution.py:25
  243.7 12.1 %fusion.2 = f32[768,1024]{1,0:T(8,128)} fusion(bf16[1024,3072]{1,0:T(8,128)(2,1)} %all-gather.2.cloned.1.call-done, f32[768,3072]{1,0:T(8,128)} %param.4, f32[768,3072]{1,0:T(8,128)} %get-tuple-element.6, f32[]{:T(128)S(6)} %sqrt.6), kind=kOutput, calls=%fused_computation.6 | convolution fusion | flops 4841275392 | bytes 28311556 | tf_op jit(solution)/shard_map/dot_general | solution.py:16
  255.8 0.0 all-reduce.5.cloned.1.call-update
  255.9 121.2 %all-reduce.5.cloned.1.call-done = f32[768,1024]{1,0:T(8,128)} async-done(((f32[768,1024]{1,0:T(8,128)}), f32[768,1024]{1,0:T(8,128)}) %all-reduce.5.cloned.1.call-update) | async-done | bytes 3145744 | tf_op jit(solution)/shard_map/psum | solution.py:19
  377.1 11.1 %multiply_reduce_fusion = (f32[]{:T(128)}, f32[768,3072]{1,0:T(8,128)}) fusion(bf16[1024,3072]{1,0:T(8,128)(2,1)} %all-gather.2.cloned.1.call-done, f32[768,1024]{1,0:T(8,128)} %all-reduce.5.cloned.1.call-done, bf16[768,1024]{1,0:T(8,128)(2,1)S(1)} %copy-done), kind=kOutput, calls=%fused_computation | convolution fusion | flops 4838916096 | bytes 20447236 | tf_op jit(solution)/shard_map/dot_general | solution.py:30
  388.2 39.4 %psum.31 = f32[]{:T(128)} all-reduce(f32[]{:T(128)} %get-tuple-element.7), channel_id=1, replica_groups=mesh['dp'=8,'mp'=4] {'dp','mp'}, use_global_device_ids=true, to_apply=%region_5.0 | all-reduce | flops 1 | bytes 8 | tf_op jit(solution)/shard_map/psum | solution.py:31
  428.3 9.0 %broadcast_divide_fusion = f32[768,3072]{1,0:T(8,128)} fusion(f32[768,3072]{1,0:T(8,128)} %get-tuple-element.8, f32[]{:T(128)S(6)} %sqrt.7), kind=kLoop, calls=%fused_computation.3 | loop fusion | flops 2359296 | bytes 18874372 | tf_op jit(solution)/shard_map/div | solution.py:32
Async XLA Ops:
  6.5 53.5 %all-gather.2.cloned.1.call-start = ((), (), s32[]{:S(2)}) async-start(), calls=%async_computation | async-start | bytes 7077888 | tf_op jit(solution)/shard_map/all_gather | solution.py:12
  11.7 180.7 %all-reduce.3.cloned.1.call-start = ((), (), s32[]{:S(2)}) async-start(), calls=%async_computation.1 | async-start | bytes 6291456 | tf_op jit(solution)/shard_map/psum | solution.py:19
  71.2 121.3 %copy-start = (bf16[768,1024]{1,0:T(8,128)(2,1)S(1)}, bf16[768,1024]{1,0:T(8,128)(2,1)}, u32[]{:S(2)}) copy-start(bf16[768,1024]{1,0:T(8,128)(2,1)} %param.5) | copy-start | bytes 4718596
  71.2 305.9 %all-reduce.5.cloned.1.call-start = ((), (), s32[]{:S(2)}) async-start(), calls=%async_computation.2 | async-start | bytes 6291456 | tf_op jit(solution)/shard_map/psum | solution.py:19
Sparse Core Ops, SparseCore 0:
  11.8 48.2 all-gather.1
  71.3 121.0 all-reduce.2
  256.0 121.0 all-reduce.4
where the time goes:
time: 444 us
  waiting for transfers between devices  291 us (66%)
  blocking collectives  79 us (18%)
  matrix products  45.4 us (10%)
  between operations  14.5 us (3%)
  other arithmetic  14.2 us (3%)
    psum x2, waiting for transfers between devices, residual_of(): summed = lax.psum(partial_out, 'mp')  242 us
    all_gather x1, waiting for transfers between devices, on_device(): everyone = lax.all_gather(hidden, 'dp', axis=0, tiled=True)  48.3 us
    psum x1, blocking collectives, on_device(): ascent_ms = lax.psum(jnp.sum(ascent * ascent), ('dp', 'mp')) / entries  39.6 us
    psum x1, blocking collectives, on_device(): descent_ms = lax.psum(jnp.sum(descent * descent), ('dp', 'mp')) / entries  39.4 us
    dot_general x2, matrix products, residual_of(): lax.dot_general(matrix, everyone, (((1,), (1,)), ((), ())), preferred_ele...  23.2 us
    dot_general x1, matrix products, on_device(): ascent = jnp.dot(resid, everyone, preferred_element_type=jnp.float32)  11.1 us
    dot_general x1, matrix products, on_device(): descent = jnp.dot(resid_two, everyone, preferred_element_type=jnp.float32)  11.1 us
    div x1, other arithmetic, on_device(): return descent / jnp.sqrt(descent_ms + epsilon)  9.05 us
  transfers between devices with their start and end apart: 3, of which 3 were waited for; matrix products, arithmetic and copies ran while one was open for 0% of the time, Pallas kernels for 0%

commit v1 on v0

--- a/solution.py
+++ b/solution.py
@@ -16,7 +16,9 @@
         partial_out = lax.dot_general(
             matrix, everyone, (((1,), (1,)), ((), ())), preferred_element_type=jnp.float32
         )
-        summed = lax.psum(partial_out, "mp")
+        summed = partial_out
+        for hop in (1, 2):
+            summed = summed + lax.ppermute(summed, "mp", [(dev, dev ^ hop) for dev in range(4)])
         result = (summed - target.astype(jnp.float32)).astype(jnp.bfloat16)
         return result
 

time: 444 us -> 614 us (1.38)
  waiting for transfers between devices: 291 us -> 452 us
  starting transfers between devices: 0.09 us -> 8.84 us
    ppermute x0 -> x4, waiting for transfers between devices: none -> 403 us  [residual_of(): lax.ppermute(summed, 'mp', [(dev, dev ^ hop) for dev in range(4)])]
    psum x2 -> x0, waiting for transfers between devices: 242 us -> none  [residual_of(): summed = lax.psum(partial_out, 'mp')]
    ppermute x0 -> x4, starting transfers between devices: none -> 8.84 us  [residual_of(): lax.ppermute(summed, 'mp', [(dev, dev ^ hop) for dev in range(4)])]
  transfers between devices with their start and end apart: 3 -> 5, of which waited for: 3 -> 5; matrix products, arithmetic and copies ran while one was open for 0% -> 0% of each run, Pallas kernels for 0% -> 0%
where the time goes in v1:
time: 614 us; the launch traced here: 613 us
  waiting for transfers between devices  452 us (74%)
  blocking collectives  77.1 us (13%)
  matrix products  43.3 us (7%)
  other arithmetic  15 us (2%)
  between operations  14.7 us (2%)
  starting transfers between devices  8.84 us (1%)
    ppermute x4, waiting for transfers between devices, residual_of(): lax.ppermute(summed, 'mp', [(dev, dev ^ hop) for dev in range(4)])  403 us
    all_gather x1, waiting for transfers between devices, on_device(): everyone = lax.all_gather(hidden, 'dp', axis=0, tiled=True)  48.4 us
    psum x1, blocking collectives, on_device(): ascent_ms = lax.psum(jnp.sum(ascent * ascent), ('dp', 'mp')) / entries  39 us
    psum x1, blocking collectives, on_device(): descent_ms = lax.psum(jnp.sum(descent * descent), ('dp', 'mp')) / entries  38.1 us
    dot_general x2, matrix products, residual_of(): lax.dot_general(matrix, everyone, (((1,), (1,)), ((), ())), preferred_ele...  21.1 us
    dot_general x1, matrix products, on_device(): ascent = jnp.dot(resid, everyone, preferred_element_type=jnp.float32)  13.1 us
  transfers between devices with their start and end apart: 5, of which 5 were waited for; matrix products, arithmetic and copies ran while one was open for 0% of the time, Pallas kernels for 0%

profile of v1, /device:TPU:0, one launch (start us, length us, event | category | flops | bytes accessed | tf_op | source)
XLA Modules:
  0.0 613.4 jit_solution(16383589734693682935)
XLA Ops:
  6.5 0.0 all-gather.2.cloned.1.call-start
  6.5 5.1 fusion.9
  11.7 0.0 all-gather.2.cloned.1.call-update
  11.7 48.4 %all-gather.2.cloned.1.call-done = bf16[1024,3072]{1,0:T(8,128)(2,1)} async-done(((bf16[128,3072]{1,0:T(8,128)(2,1)}), bf16[1024,3072]{1,0:T(8,128)(2,1)}) %all-gather.2.cloned.1.call-update) | async-done | bytes 6291472 | tf_op jit(solution)/shard_map/all_gather | solution.py:12
  60.1 9.5 %fusion.5 = f32[768,1024]{0,1:T(8,128)S(1)} fusion(bf16[1024,3072]{1,0:T(8,128)(2,1)} %all-gather.2.cloned.1.call-done, f32[768,3072]{1,0:T(8,128)} %param.4), kind=kOutput, calls=%fused_computation.14 | convolution fusion | flops 4834197504 | bytes 18874368 | tf_op jit(solution)/shard_map/dot_general | solution.py:16
  69.6 1.6 collective-permute-start
  71.2 68.8 %collective-permute-done = f32[768,1024]{0,1:T(8,128)S(1)} collective-permute-done((f32[768,1024]{0,1:T(8,128)S(1)}, f32[768,1024]{0,1:T(8,128)S(1)}, u32[]{:S(2)}, u32[]{:S(2)}) %collective-permute-start) | collective-permute-done | bytes 3145760 | tf_op jit(solution)/shard_map/ppermute | solution.py:21
  140.0 0.4 add.25
  140.3 0.0 copy-start.1
  140.4 2.5 collective-permute-start.1
  142.8 2.6 copy.4
  145.4 0.0 copy-done.1
  145.4 132.8 %collective-permute-done.1 = f32[768,1024]{0,1:T(8,128)} collective-permute-done((f32[768,1024]{0,1:T(8,128)S(1)}, f32[768,1024]{0,1:T(8,128)}, u32[]{:S(2)}, u32[]{:S(2)}) %collective-permute-start.1) | collective-permute-done | bytes 3145760 | tf_op jit(solution)/shard_map/ppermute | solution.py:21
  278.3 0.0 slice-start
  278.3 13.1 %multiply_reduce_fusion.1 = (f32[]{:T(128)}, f32[768,3072]{1,0:T(8,128)}) fusion(bf16[1024,3072]{1,0:T(8,128)(2,1)} %all-gather.2.cloned.1.call-done, bf16[768,1024]{0,1:T(8,128)(2,1)} %copy.4, f32[768,1024]{0,1:T(8,128)} %copy-done.1, f32[768,1024]{0,1:T(8,128)} %collective-permute-done.1), kind=kOutput, calls=%fused_computation.2 | convolution fusion | flops 4839702528 | bytes 23592964 | tf_op jit(solution)/shard_map/dot_general | solution.py:26
  291.4 39.0 %psum.14 = f32[]{:T(128)} all-reduce(f32[]{:T(128)} %get-tuple-element.5), channel_id=1, replica_groups=mesh['dp'=8,'mp'=4] {'dp','mp'}, use_global_device_ids=true, to_apply=%region_1.0 | all-reduce | flops 1 | bytes 8 | tf_op jit(solution)/shard_map/psum | solution.py:27
  331.0 0.0 slice-start.1
  331.0 11.6 %fusion.2 = f32[768,1024]{0,1:T(8,128)S(1)} fusion(bf16[1024,3072]{1,0:T(8,128)(2,1)} %all-gather.2.cloned.1.call-done, f32[768,3072]{1,0:T(8,128)} %param.4, f32[768,3072]{1,0:T(8,128)} %get-tuple-element.6, f32[]{:T(128)S(6)} %sqrt.6), kind=kOutput, calls=%fused_computation.6 | convolution fusion | flops 4841275392 | bytes 28311556 | tf_op jit(solution)/shard_map/dot_general | solution.py:16
  342.6 0.0 copy-start
  342.6 2.2 collective-permute-start.2
  344.8 67.5 %collective-permute-done.2 = f32[768,1024]{0,1:T(8,128)S(1)} collective-permute-done((f32[768,1024]{0,1:T(8,128)S(1)}, f32[768,1024]{0,1:T(8,128)S(1)}, u32[]{:S(2)}, u32[]{:S(2)}) %collective-permute-start.2) | collective-permute-done | bytes 3145760 | tf_op jit(solution)/shard_map/ppermute | solution.py:21
  412.3 0.4 add.29
  412.7 2.6 collective-permute-start.3
  415.3 134.3 %collective-permute-done.3 = f32[768,1024]{0,1:T(8,128)S(1)} collective-permute-done((f32[768,1024]{0,1:T(8,128)S(1)}, f32[768,1024]{0,1:T(8,128)S(1)}, u32[]{:S(2)}, u32[]{:S(2)}) %collective-permute-start.3) | collective-permute-done | bytes 3145760 | tf_op jit(solution)/shard_map/ppermute | solution.py:21
  549.6 0.0 slice-done
  549.6 0.0 slice-done.1
  549.6 0.0 copy-done
  549.7 9.1 %multiply_reduce_fusion = (f32[]{:T(128)}, f32[768,3072]{1,0:T(8,128)}) fusion(bf16[1024,3072]{1,0:T(8,128)(2,1)S(1)} %bitcast.7, bf16[768,1024]{0,1:T(8,128)(2,1)S(1)} %copy-done, f32[768,1024]{0,1:T(8,128)S(1)} %add.29, f32[768,1024]{0,1:T(8,128)S(1)} %collective-permute-done.3), kind=kOutput, calls=%fused_computation | convolution fusion | flops 4839702528 | bytes 23592964 | tf_op jit(solution)/shard_map/dot_general | solution.py:32
  558.7 38.1 %psum.15 = f32[]{:T(128)} all-reduce(f32[]{:T(128)} %get-tuple-element.7), channel_id=1, replica_groups=mesh['dp'=8,'mp'=4] {'dp','mp'}, use_global_device_ids=true, to_apply=%region_3.0 | all-reduce | flops 1 | bytes 8 | tf_op jit(solution)/shard_map/psum | solution.py:33
  597.5 9.0 %broadcast_divide_fusion = f32[768,3072]{1,0:T(8,128)} fusion(f32[768,3072]{1,0:T(8,128)} %get-tuple-element.8, f32[]{:T(128)S(6)} %sqrt.7), kind=kLoop, calls=%fused_computation.3 | loop fusion | flops 2359296 | bytes 18874372 | tf_op jit(solution)/shard_map/div | solution.py:34
  (1 shorter events, 0.0 us)
Async XLA Ops:
  6.5 53.5 %all-gather.2.cloned.1.call-start = ((), (), s32[]{:S(2)}) async-start(), calls=%async_computation | async-start | bytes 7077888 | tf_op jit(solution)/shard_map/all_gather | solution.py:12
  69.6 70.3 %collective-permute-start = (f32[768,1024]{0,1:T(8,128)S(1)}, f32[768,1024]{0,1:T(8,128)S(1)}, u32[]{:S(2)}, u32[]{:S(2)}) collective-permute-start(f32[768,1024]{0,1:T(8,128)S(1)} %fusion.5), channel_id=1, source_target_pairs={{0,1},{1,0},{2,3},{3,2},{4,5},{5,4},{6,7},{7,6},{8,9},{9,8},{10,11... | collective-permute-start | bytes 9437192 | tf_op jit(solution)/shard_map/ppermute | solution.py:21
  140.3 5.1 copy-start.1
  140.4 137.9 %collective-permute-start.1 = (f32[768,1024]{0,1:T(8,128)S(1)}, f32[768,1024]{0,1:T(8,128)}, u32[]{:S(2)}, u32[]{:S(2)}) collective-permute-start(f32[768,1024]{0,1:T(8,128)S(1)} %add.25), channel_id=1, source_target_pairs={{0,2},{1,3},{2,0},{3,1},{4,6},{5,7},{6,4},{7,5},{8,10},{9,11},{10,... | collective-permute-start | bytes 9437192 | tf_op jit(solution)/shard_map/ppermute | solution.py:21
  278.3 271.3 %slice-start = ((s8[6291456]{0:T(1024)(128)(4,1)}), s8[2097152]{0:T(1024)(128)(4,1)S(1)}, s32[]{:S(2)}) async-start(s8[6291456]{0:T(1024)(128)(4,1)} %bitcast.6), calls=%async_computation.1 | async-start | bytes 4194304
  331.0 218.7 %slice-start.1 = ((s8[6291456]{0:T(1024)(128)(4,1)}), s8[4194304]{0:T(1024)(128)(4,1)S(1)}, s32[]{:S(2)}) async-start(s8[6291456]{0:T(1024)(128)(4,1)} %bitcast.6), calls=%async_computation.2 | async-start | bytes 8388608
  342.6 207.0 %copy-start = (bf16[768,1024]{0,1:T(8,128)(2,1)S(1)}, bf16[768,1024]{0,1:T(8,128)(2,1)}, u32[]{:S(2)}) copy-start(bf16[768,1024]{0,1:T(8,128)(2,1)} %copy.4) | copy-start | bytes 4718596
  342.6 69.7 %collective-permute-start.2 = (f32[768,1024]{0,1:T(8,128)S(1)}, f32[768,1024]{0,1:T(8,128)S(1)}, u32[]{:S(2)}, u32[]{:S(2)}) collective-permute-start(f32[768,1024]{0,1:T(8,128)S(1)} %fusion.2), channel_id=1, source_target_pairs={{0,1},{1,0},{2,3},{3,2},{4,5},{5,4},{6,7},{7,6},{8,9},{9,8},{10,11... | collective-permute-start | bytes 9437192 | tf_op jit(solution)/shard_map/ppermute | solution.py:21
  412.7 136.9 %collective-permute-start.3 = (f32[768,1024]{0,1:T(8,128)S(1)}, f32[768,1024]{0,1:T(8,128)S(1)}, u32[]{:S(2)}, u32[]{:S(2)}) collective-permute-start(f32[768,1024]{0,1:T(8,128)S(1)} %add.29), channel_id=1, source_target_pairs={{0,2},{1,3},{2,0},{3,1},{4,6},{5,7},{6,4},{7,5},{8,10},{9,11},{10,... | collective-permute-start | bytes 9437192 | tf_op jit(solution)/shard_map/ppermute | solution.py:21
Sparse Core Ops, SparseCore 0:
  11.8 48.2 all-gather.1
